TPU v7x, 32 devices: a whole 2x2x4 slice. The times are simulated.
32 devices in a mesh: groups: 2 (over x), zonal: 16 (over z, y, core).
Axes of the slice: x: 2, y: 2, z: 4, core: 2. Of those that a mesh axis runs over, the one named last changes fastest.
Arguments:
- field: bfloat16 [192, 32, 2048], P('groups', None, 'zonal'), parts along dimension 0, may hold values from -6 to 6
- land_mask: int32 [32, 2048], P(None, 'zonal'), may hold values from 0 to 1, as said below
- dw_weight: float32 [2, 49, 96], replicated, may hold values from -0.875 to 0.875
- ln_gain: float32 [2, 96], replicated, may hold values from 0.1 to 1.9
- ln_shift: float32 [2, 96], replicated, may hold values from -3 to 3
- w_in: bfloat16 [2, 384, 96], replicated, may hold values from -0.625 to 0.625
- b_in: float32 [2, 384], replicated, may hold values from -3 to 3
- w_out: bfloat16 [2, 96, 384], replicated, may hold values from -0.3125 to 0.3125
Outputs:
- evolved: bfloat16 [192, 32, 2048], P('groups', None, 'zonal'), parts along dimension 0
There are 2 independent parts, one for each index of `groups`. A program takes and returns all parts, laid end to end along the dimension named above; an argument that names none is the same for every part. Nothing has to cross between parts.
Inputs may be any that keep to these rules, and one draw needn't show every extreme that they name: `land_mask`: 1 marks an ocean cell, 0 a land cell.
All inputs are finite; a program needn't handle non-finite values.
Results may differ from a plain program's by a relative error of at most 0.0058.
Values may be sent and summed in bfloat16 or wider, within the bound.
A program may use at most 64 MiB of HBM per device.

v0:
```python
import jax
import jax.numpy as jnp
from jax import lax
from jax.sharding import PartitionSpec as P


def swapped(value, axis, bit):
    return lax.ppermute(value, axis, [(i, i ^ 1 << bit) for i in range(lax.axis_size(axis))])


def extended_2(cells, sides, width):
    for axis, dim in sides:
        count = lax.axis_size(axis)
        head = lax.slice_in_dim(cells, 0, width, axis=dim)
        tail = lax.slice_in_dim(cells, cells.shape[dim] - width, cells.shape[dim], axis=dim)
        cells = jnp.concatenate(
            [
                lax.ppermute(tail, axis, [(i, (i + 1) % count) for i in range(count)]),
                cells,
                lax.ppermute(head, axis, [((i + 1) % count, i) for i in range(count)]),
            ],
            axis=dim,
        )
    return cells


def add_fold(extended):
    top = extended[:, -3:, ::-1][:, ::-1, :]
    digits = lax.axis_size("zonal").bit_length() - 1
    for bit in range(digits):
        top = swapped(top, "zonal", bit)
    south = jnp.zeros((extended.shape[0], 3, extended.shape[2]), extended.dtype)
    return jnp.concatenate([south, extended, top], axis=1)


def run_block(padded, center, mask_wide, kernel, gain, shift, wa, ba, wb):
    channels, rows, width = center.shape

    def compute():
        conv = jnp.zeros((channels, 32, width), jnp.float32)
        for p in range(7):
            for q in range(7):
                conv = (
                    conv + kernel[7 * p + q][:, None, None] * padded[:, p : p + 32, q : q + width]
                )
        mean = jnp.mean(conv, axis=0)
        cent = conv - mean
        var = jnp.mean(cent * cent, axis=0)
        normed = (
            cent * lax.rsqrt(var + 1e-06) * gain[:, None, None] + shift[:, None, None]
        ).astype(jnp.bfloat16)
        flat = normed.reshape(channels, -1)
        hidden = jnp.dot(wa, flat, preferred_element_type=jnp.float32) + ba[:, None]
        hidden = jax.nn.gelu(hidden, approximate=True).astype(jnp.bfloat16)
        outer = jnp.dot(wb, hidden, preferred_element_type=jnp.float32).reshape(channels, 32, width)
        return (mask_wide.astype(jnp.float32)[None] * (center.astype(jnp.float32) + outer)).astype(
            jnp.bfloat16
        )

    def rowblock(index, out):
        res = compute()
        return res

    return lax.fori_loop(0, rows // 32, rowblock, jnp.zeros(center.shape, jnp.bfloat16))


def local(field, land_mask, dw_weight, ln_gain, ln_shift, w_in, b_in, w_out):
    state = field * land_mask.astype(jnp.bfloat16)[None]
    wide = extended_2(state, (("zonal", 2),), 6)
    mask_wide = extended_2(land_mask, (("zonal", 1),), 3)
    first = run_block(
        add_fold(wide),
        wide[:, :, 3:-3],
        mask_wide,
        dw_weight[0],
        ln_gain[0],
        ln_shift[0],
        w_in[0],
        b_in[0],
        w_out[0],
    )
    state = run_block(
        add_fold(first),
        first[:, :, 3:-3],
        land_mask,
        dw_weight[1],
        ln_gain[1],
        ln_shift[1],
        w_in[1],
        b_in[1],
        w_out[1],
    )
    return state


def solution(mesh):
    placed = (P("groups", None, "zonal"), P(None, "zonal"), P(), P(), P(), P(), P(), P())
    return jax.shard_map(
        local, mesh=mesh, in_specs=placed, out_specs=P("groups", None, "zonal"), check_vma=False
    )
```

profile of v0, /device:TPU:0, one launch (start us, length us, event | category | flops | bytes accessed | tf_op | source)
XLA Modules:
  0.0 123.2 jit_solution(14273417761980652233)
XLA Ops:
  0.8 1.8 %copy.9 = bf16[96,32,128]{0,2,1:T(8,128)(2,1)S(1)} copy(bf16[96,32,128]{2,1,0:T(8,128)(2,1)} %param.8) | data formatting | bytes 1572864 | tf_op args[0]
  3.9 5.0 %collective-permute-start.3 = (bf16[96,32,6]{0,2,1:T(8,128)(2,1)S(1)}, bf16[96,32,6]{0,2,1:T(8,128)(2,1)S(1)}, u32[]{:S(2)}, u32[]{:S(2)}) collective-permute-start(bf16[96,32,6]{0,2,1:T(8,128)(2,1)S(1)} %get-tuple-element.56), channel_id=1, source_target_pairs={{1,0},{2,1},{3,2},{4,3},{5,4},{6,5},{7,6},{8,7},{9,8},{10,9},{11,1... | collective-permute-start | bytes 110600 | tf_op jit(solution)/shard_map/ppermute | solution.py:20
  9.1 4.4 %collective-permute-start.1 = (s32[32,3]{1,0:T(8,128)S(1)}, s32[32,3]{1,0:T(8,128)S(1)}, u32[]{:S(2)}, u32[]{:S(2)}) collective-permute-start(s32[32,3]{1,0:T(8,128)S(1)} %get-tuple-element.184), channel_id=1, source_target_pairs={{1,0},{2,1},{3,2},{4,3},{5,4},{6,5},{7,6},{8,7},{9,8},{10,9},{11,1... | collective-permute-start | bytes 1160 | tf_op jit(solution)/shard_map/ppermute | solution.py:20
  16.0 5.1 %collective-permute-done.5 = bf16[96,3,140]{0,2,1:T(8,128)(2,1)S(1)} collective-permute-done((bf16[96,3,140]{0,2,1:T(8,128)(2,1)S(1)}, bf16[96,3,140]{0,2,1:T(8,128)(2,1)S(1)}, u32[]{:S(2)}, u32[]{:S(2)}) %collective-permute-start.5) | collective-permute-done | bytes 80672 | tf_op jit(solution)/shard_map/ppermute | solution.py:8
  21.1 4.7 %collective-permute-done.6 = bf16[96,3,140]{0,2,1:T(8,128)(2,1)S(1)} collective-permute-done((bf16[96,3,140]{0,2,1:T(8,128)(2,1)S(1)}, bf16[96,3,140]{0,2,1:T(8,128)(2,1)S(1)}, u32[]{:S(2)}, u32[]{:S(2)}) %collective-permute-start.6) | collective-permute-done | bytes 80672 | tf_op jit(solution)/shard_map/ppermute | solution.py:8
  25.9 6.2 %collective-permute-done.7 = bf16[96,3,140]{0,2,1:T(8,128)(2,1)S(1)} collective-permute-done((bf16[96,3,140]{0,2,1:T(8,128)(2,1)S(1)}, bf16[96,3,140]{0,2,1:T(8,128)(2,1)S(1)}, u32[]{:S(2)}, u32[]{:S(2)}) %collective-permute-start.7) | collective-permute-done | bytes 80672 | tf_op jit(solution)/shard_map/ppermute | solution.py:8
  32.5 17.7 %fusion.113 = (f32[32,134]{1,0:T(8,128)S(1)}, f32[96,32,134]{0,2,1:T(8,128)S(1)}) fusion(bf16[96,35,140]{0,2,1:T(8,128)(2,1)S(1)} %pad_maximum_fusion, f32[96]{0:T(128)S(1)} %get-tuple-element.130, f32[96]{0:T(128)S(1)} %get-tuple-element.131, f32[96]{0:T(128)S(1)} %get-tuple-element.132, f32[96]{0:T(128)S(1)} %get-tuple-element.133, ...), kind=kLoop, calls=%fused_computation.281 | loop fusion | flops 62977856 | bytes 33015040 | tf_op jit(solution)/shard_map/while/body/eval_jaxpr/reduce_sum | solution.py:46
  50.3 1.9 %multiply_reduce_fusion = f32[32,134]{1,0:T(8,128)S(1)} fusion(f32[96,32,134]{0,2,1:T(8,128)S(1)} %get-tuple-element.54, f32[32,134]{1,0:T(8,128)S(1)} %broadcast_multiply_fusion.1), kind=kLoop, calls=%fused_computation.74 | loop fusion | flops 1230656 | bytes 1680896 | tf_op jit(solution)/shard_map/while/body/eval_jaxpr/reduce_sum | solution.py:48
  52.3 1.3 %add_convert_fusion = bf16[96,32,134]{0,2,1:T(8,128)(2,1)S(1)} fusion(f32[96,32,134]{0,2,1:T(8,128)S(1)} %get-tuple-element.54, f32[96]{0:T(128)S(1)} %get-tuple-element.188, f32[96]{0:T(128)S(1)} %get-tuple-element.189, f32[32,134]{1,0:T(8,128)S(1)} %add_rsqrt_fusion, f32[32,134]{1,0:T(8,128)S(1)} %broadcast_multiply_fusion.1), kind=kLoop, calls=%fused_computation.73 | loop fusion | flops 2058240 | bytes 2504960 | tf_op jit(solution)/shard_map/while/body/eval_jaxpr/convert_element_type | solution.py:51
  54.8 5.2 %convolution_bitcast_fusion = f32[96,4288]{1,0:T(8,128)} fusion(bf16[96,4288]{0,1:T(8,128)(2,1)} %reshape.356, f32[384]{0:T(512)S(1)} %get-tuple-element.50, bf16[2,96,384]{2,1,0:T(8,128)(2,1)S(1)} %copy-done.5, bf16[2,384,96]{1,2,0:T(8,128)(2,1)S(1)} %copy-done.7), kind=kOutput, calls=%fused_computation.40 | convolution fusion | flops 648757248 | bytes 2619392 | tf_op jit(solution)/shard_map/while/body/eval_jaxpr/dot_general | solution.py:55
  60.0 2.9 %copy.10 = f32[96,4288]{0,1:T(8,128)} copy(f32[96,4288]{1,0:T(8,128)} %convolution_bitcast_fusion) | data formatting | bytes 3293184 | tf_op jit(solution)/shard_map/while/body/eval_jaxpr/dot_general | solution.py:55
  62.9 2.7 %reshape.357 = f32[96,32,134]{0,2,1:T(8,128)} reshape(f32[96,4288]{0,1:T(8,128)} %copy.10) | data formatting | bytes 3293184 | tf_op jit(solution)/shard_map/while/body/eval_jaxpr/reshape | solution.py:55
  65.6 2.0 %fusion.43 = bf16[96,32,134]{0,2,1:T(8,128)(2,1)S(1)} fusion(f32[96,32,134]{0,2,1:T(8,128)} %reshape.357, f32[32,134]{1,0:T(8,128)S(1)} %add_convert_fusion.2, bf16[96,32,140]{0,2,1:T(8,128)(2,1)S(1)} %pad_maximum_fusion.1), kind=kLoop, calls=%fused_computation.72 | loop fusion | flops 1646592 | bytes 3310336 | tf_op jit(solution)/shard_map/while/body/eval_jaxpr/convert_element_type | solution.py:56
  68.2 1.3 %collective-permute-done.8 = bf16[96,3,134]{0,2,1:T(8,128)(2,1)S(1)} collective-permute-done((bf16[96,3,134]{0,2,1:T(8,128)(2,1)S(1)}, bf16[96,3,134]{0,2,1:T(8,128)(2,1)S(1)}, u32[]{:S(2)}, u32[]{:S(2)}) %collective-permute-start.8) | collective-permute-done | bytes 77216 | tf_op jit(solution)/shard_map/ppermute | solution.py:8
  70.0 4.5 %collective-permute-done.9 = bf16[96,3,134]{0,2,1:T(8,128)(2,1)S(1)} collective-permute-done((bf16[96,3,134]{0,2,1:T(8,128)(2,1)S(1)}, bf16[96,3,134]{0,2,1:T(8,128)(2,1)S(1)}, u32[]{:S(2)}, u32[]{:S(2)}) %collective-permute-start.9) | collective-permute-done | bytes 77216 | tf_op jit(solution)/shard_map/ppermute | solution.py:8
  74.5 4.7 %collective-permute-done.10 = bf16[96,3,134]{0,2,1:T(8,128)(2,1)S(1)} collective-permute-done((bf16[96,3,134]{0,2,1:T(8,128)(2,1)S(1)}, bf16[96,3,134]{0,2,1:T(8,128)(2,1)S(1)}, u32[]{:S(2)}, u32[]{:S(2)}) %collective-permute-start.10) | collective-permute-done | bytes 77216 | tf_op jit(solution)/shard_map/ppermute | solution.py:8
  79.2 6.1 %collective-permute-done.11 = bf16[96,3,134]{0,2,1:T(8,128)(2,1)S(1)} collective-permute-done((bf16[96,3,134]{0,2,1:T(8,128)(2,1)S(1)}, bf16[96,3,134]{0,2,1:T(8,128)(2,1)S(1)}, u32[]{:S(2)}, u32[]{:S(2)}) %collective-permute-start.11) | collective-permute-done | bytes 77216 | tf_op jit(solution)/shard_map/ppermute | solution.py:8
  85.3 25.4 %fusion.111 = (f32[32,128]{1,0:T(8,128)S(1)}, f32[96,32,128]{0,2,1:T(8,128)S(1)}) fusion(bf16[96,3,134]{0,2,1:T(8,128)(2,1)S(1)} %collective-permute-done.11, bf16[96,32,134]{0,2,1:T(8,128)(2,1)S(1)} %fusion.43, f32[96]{0:T(128)S(1)} %get-tuple-element.159, f32[96]{0:T(128)S(1)} %get-tuple-element.140, f32[96]{0:T(128)S(1)} %get-tuple-element.58, ...), kind=kLoop, calls=%fused_computation.280 | loop fusion | flops 82571264 | bytes 10172928 | tf_op jit(solution)/shard_map/while/body/eval_jaxpr/reduce_sum | solution.py:46
  110.7 1.3 %multiply_reduce_fusion.1 = f32[32,128]{1,0:T(8,128)S(1)} fusion(f32[96,32,128]{0,2,1:T(8,128)S(1)} %get-tuple-element.52, f32[32,128]{1,0:T(8,128)S(1)} %broadcast_multiply_fusion.2), kind=kLoop, calls=%fused_computation.103 | loop fusion | flops 1175552 | bytes 1605632 | tf_op jit(solution)/shard_map/while/body/eval_jaxpr/reduce_sum | solution.py:48
  112.1 1.4 %add_convert_fusion.1 = bf16[96,32,128]{0,2,1:T(8,128)(2,1)S(1)} fusion(f32[96,32,128]{0,2,1:T(8,128)S(1)} %get-tuple-element.52, f32[96]{0:T(128)S(1)} %get-tuple-element.187, f32[96]{0:T(128)S(1)} %get-tuple-element.190, f32[32,128]{1,0:T(8,128)S(1)} %add_rsqrt_fusion.1, f32[32,128]{1,0:T(8,128)S(1)} %broadcast_multiply_fusion.2), kind=kLoop, calls=%fused_computation.102 | loop fusion | flops 1966080 | bytes 2392832 | tf_op jit(solution)/shard_map/while/body/eval_jaxpr/convert_element_type | solution.py:51
  113.6 3.9 %convolution_bitcast_fusion.1 = f32[96,4096]{1,0:T(8,128)} fusion(bf16[96,4096]{0,1:T(8,128)(2,1)S(1)} %bitcast.243, f32[384]{0:T(512)S(1)} %get-tuple-element.49, bf16[2,96,384]{2,1,0:T(8,128)(2,1)S(1)} %copy-done.6, bf16[2,384,96]{1,2,0:T(8,128)(2,1)S(1)} %copy-done.8), kind=kOutput, calls=%fused_computation.41 | convolution fusion | flops 619708416 | bytes 2770944 | tf_op jit(solution)/shard_map/while/body/eval_jaxpr/dot_general | solution.py:55
  117.4 1.8 %copy.13 = f32[96,4096]{0,1:T(8,128)S(1)} copy(f32[96,4096]{1,0:T(8,128)} %convolution_bitcast_fusion.1) | data formatting | bytes 3145728 | tf_op jit(solution)/shard_map/while/body/eval_jaxpr/reshape | solution.py:55
  119.3 1.5 %fusion.70 = bf16[96,32,128]{0,2,1:T(8,128)(2,1)} fusion(f32[96,32,128]{0,2,1:T(8,128)S(1)} %bitcast.242, f32[32,128]{1,0:T(8,128)S(1)} %get-tuple-element.181, bf16[96,32,134]{0,2,1:T(8,128)(2,1)S(1)} %fusion.43), kind=kLoop, calls=%fused_computation.101 | loop fusion | flops 1572864 | bytes 3162112 | tf_op jit(solution)/shard_map/while/body/eval_jaxpr/convert_element_type | solution.py:56
  120.8 2.4 %copy.12 = bf16[96,32,128]{2,1,0:T(8,128)(2,1)} copy(bf16[96,32,128]{0,2,1:T(8,128)(2,1)} %fusion.70) | data formatting | bytes 1572864 | tf_op jit(solution)/shard_map/while/body/eval_jaxpr/convert_element_type | solution.py:56
  (57 shorter events, 7.4 us)
Async XLA Ops:
  0.8 8.2 %copy-start = (s32[32,128]{1,0:T(8,128)S(1)}, s32[32,128]{1,0:T(8,128)}, u32[]{:S(2)}) copy-start(s32[32,128]{1,0:T(8,128)} %param.9) | copy-start | bytes 49156
  0.8 12.7 %copy-start.1 = (f32[2,49,96]{2,0,1:T(2,128)S(1)}, f32[2,49,96]{2,0,1:T(2,128)}, u32[]{:S(2)}) copy-start(f32[2,49,96]{2,0,1:T(2,128)} %param.10) | copy-start | bytes 112900
  3.3 11.3 %copy-start.3 = (f32[2,96]{1,0:T(2,128)S(1)}, f32[2,96]{1,0:T(2,128)}, u32[]{:S(2)}) copy-start(f32[2,96]{1,0:T(2,128)} %param.12) | copy-start | bytes 2308
  3.3 11.3 %copy-start.4 = (f32[2,96]{1,0:T(2,128)S(1)}, f32[2,96]{1,0:T(2,128)}, u32[]{:S(2)}) copy-start(f32[2,96]{1,0:T(2,128)} %param.11) | copy-start | bytes 2308
  3.3 17.7 %copy-start.2 = (f32[2,384]{1,0:T(2,128)S(1)}, f32[2,384]{1,0:T(2,128)}, u32[]{:S(2)}) copy-start(f32[2,384]{1,0:T(2,128)} %param.14) | copy-start | bytes 9220
  3.4 10.2 %collective-permute-start.2 = (bf16[96,32,6]{0,2,1:T(8,128)(2,1)S(1)}, bf16[96,32,6]{0,2,1:T(8,128)(2,1)S(1)}, u32[]{:S(2)}, u32[]{:S(2)}) collective-permute-start(bf16[96,32,6]{0,2,1:T(8,128)(2,1)S(1)} %get-tuple-element.55), channel_id=1, source_target_pairs={{0,1},{1,2},{2,3},{3,4},{4,5},{5,6},{6,7},{7,8},{8,9},{9,10},{10,1... | collective-permute-start | bytes 110600 | tf_op jit(solution)/shard_map/ppermute | solution.py:18
  3.9 9.6 %collective-permute-start.3 = (bf16[96,32,6]{0,2,1:T(8,128)(2,1)S(1)}, bf16[96,32,6]{0,2,1:T(8,128)(2,1)S(1)}, u32[]{:S(2)}, u32[]{:S(2)}) collective-permute-start(bf16[96,32,6]{0,2,1:T(8,128)(2,1)S(1)} %get-tuple-element.56), channel_id=1, source_target_pairs={{1,0},{2,1},{3,2},{4,3},{5,4},{6,5},{7,6},{8,7},{9,8},{10,9},{11,1... | collective-permute-start | bytes 110600 | tf_op jit(solution)/shard_map/ppermute | solution.py:20
  9.1 16.8 %collective-permute-start = (s32[32,3]{1,0:T(8,128)S(1)}, s32[32,3]{1,0:T(8,128)S(1)}, u32[]{:S(2)}, u32[]{:S(2)}) collective-permute-start(s32[32,3]{1,0:T(8,128)S(1)} %get-tuple-element.183), channel_id=1, source_target_pairs={{0,1},{1,2},{2,3},{3,4},{4,5},{5,6},{6,7},{7,8},{8,9},{9,10},{10,1... | collective-permute-start | bytes 1160 | tf_op jit(solution)/shard_map/ppermute | solution.py:18
  9.1 16.8 %collective-permute-start.1 = (s32[32,3]{1,0:T(8,128)S(1)}, s32[32,3]{1,0:T(8,128)S(1)}, u32[]{:S(2)}, u32[]{:S(2)}) collective-permute-start(s32[32,3]{1,0:T(8,128)S(1)} %get-tuple-element.184), channel_id=1, source_target_pairs={{1,0},{2,1},{3,2},{4,3},{5,4},{6,5},{7,6},{8,7},{9,8},{10,9},{11,1... | collective-permute-start | bytes 1160 | tf_op jit(solution)/shard_map/ppermute | solution.py:20
  14.6 1.4 %collective-permute-start.4 = (bf16[96,3,140]{0,2,1:T(8,128)(2,1)S(1)}, bf16[96,3,140]{0,2,1:T(8,128)(2,1)S(1)}, u32[]{:S(2)}, u32[]{:S(2)}) collective-permute-start(bf16[96,3,140]{0,2,1:T(8,128)(2,1)S(1)} %rev.8), channel_id=1, source_target_pairs={{0,1},{1,0},{2,3},{3,2},{4,5},{5,4},{6,7},{7,6},{8,9},{9,8},{10,11... | collective-permute-start | bytes 241928 | tf_op jit(solution)/shard_map/ppermute | solution.py:8
  16.0 5.1 %collective-permute-start.5 = (bf16[96,3,140]{0,2,1:T(8,128)(2,1)S(1)}, bf16[96,3,140]{0,2,1:T(8,128)(2,1)S(1)}, u32[]{:S(2)}, u32[]{:S(2)}) collective-permute-start(bf16[96,3,140]{0,2,1:T(8,128)(2,1)S(1)} %collective-permute-done.4), channel_id=1, source_target_pairs={{0,2},{1,3},{2,0},{3,1},{4,6},{5,7},{6,4},{7,5},{8,10},{9,11},{10,... | collective-permute-start | bytes 241928 | tf_op jit(solution)/shard_map/ppermute | solution.py:8
  21.1 4.7 %collective-permute-start.6 = (bf16[96,3,140]{0,2,1:T(8,128)(2,1)S(1)}, bf16[96,3,140]{0,2,1:T(8,128)(2,1)S(1)}, u32[]{:S(2)}, u32[]{:S(2)}) collective-permute-start(bf16[96,3,140]{0,2,1:T(8,128)(2,1)S(1)} %collective-permute-done.5), channel_id=1, source_target_pairs={{0,4},{1,5},{2,6},{3,7},{4,0},{5,1},{6,2},{7,3},{8,12},{9,13},{10,... | collective-permute-start | bytes 241928 | tf_op jit(solution)/shard_map/ppermute | solution.py:8
  25.8 6.3 %collective-permute-start.7 = (bf16[96,3,140]{0,2,1:T(8,128)(2,1)S(1)}, bf16[96,3,140]{0,2,1:T(8,128)(2,1)S(1)}, u32[]{:S(2)}, u32[]{:S(2)}) collective-permute-start(bf16[96,3,140]{0,2,1:T(8,128)(2,1)S(1)} %collective-permute-done.6), channel_id=1, source_target_pairs={{0,8},{1,9},{2,10},{3,11},{4,12},{5,13},{6,14},{7,15},{8,0},{9,1},... | collective-permute-start | bytes 241928 | tf_op jit(solution)/shard_map/ppermute | solution.py:8
  52.2 2.5 %copy-start.5 = (bf16[2,96,384]{2,1,0:T(8,128)(2,1)S(1)}, bf16[2,96,384]{2,1,0:T(8,128)(2,1)}, u32[]{:S(2)}) copy-start(bf16[2,96,384]{2,1,0:T(8,128)(2,1)} %param.15) | copy-start | bytes 442372
  52.3 2.5 %copy-start.7 = (bf16[2,384,96]{1,2,0:T(8,128)(2,1)S(1)}, bf16[2,384,96]{1,2,0:T(8,128)(2,1)}, u32[]{:S(2)}) copy-start(bf16[2,384,96]{1,2,0:T(8,128)(2,1)} %param.13) | copy-start | bytes 442372
  68.2 1.4 %collective-permute-start.8 = (bf16[96,3,134]{0,2,1:T(8,128)(2,1)S(1)}, bf16[96,3,134]{0,2,1:T(8,128)(2,1)S(1)}, u32[]{:S(2)}, u32[]{:S(2)}) collective-permute-start(bf16[96,3,134]{0,2,1:T(8,128)(2,1)S(1)} %rev.9), channel_id=1, source_target_pairs={{0,1},{1,0},{2,3},{3,2},{4,5},{5,4},{6,7},{7,6},{8,9},{9,8},{10,11... | collective-permute-start | bytes 231560 | tf_op jit(solution)/shard_map/ppermute | solution.py:8
  69.5 5.0 %collective-permute-start.9 = (bf16[96,3,134]{0,2,1:T(8,128)(2,1)S(1)}, bf16[96,3,134]{0,2,1:T(8,128)(2,1)S(1)}, u32[]{:S(2)}, u32[]{:S(2)}) collective-permute-start(bf16[96,3,134]{0,2,1:T(8,128)(2,1)S(1)} %collective-permute-done.8), channel_id=1, source_target_pairs={{0,2},{1,3},{2,0},{3,1},{4,6},{5,7},{6,4},{7,5},{8,10},{9,11},{10,... | collective-permute-start | bytes 231560 | tf_op jit(solution)/shard_map/ppermute | solution.py:8
  74.5 4.7 %collective-permute-start.10 = (bf16[96,3,134]{0,2,1:T(8,128)(2,1)S(1)}, bf16[96,3,134]{0,2,1:T(8,128)(2,1)S(1)}, u32[]{:S(2)}, u32[]{:S(2)}) collective-permute-start(bf16[96,3,134]{0,2,1:T(8,128)(2,1)S(1)} %collective-permute-done.9), channel_id=1, source_target_pairs={{0,4},{1,5},{2,6},{3,7},{4,0},{5,1},{6,2},{7,3},{8,12},{9,13},{10,... | collective-permute-start | bytes 231560 | tf_op jit(solution)/shard_map/ppermute | solution.py:8
  79.2 6.1 %collective-permute-start.11 = (bf16[96,3,134]{0,2,1:T(8,128)(2,1)S(1)}, bf16[96,3,134]{0,2,1:T(8,128)(2,1)S(1)}, u32[]{:S(2)}, u32[]{:S(2)}) collective-permute-start(bf16[96,3,134]{0,2,1:T(8,128)(2,1)S(1)} %collective-permute-done.10), channel_id=1, source_target_pairs={{0,8},{1,9},{2,10},{3,11},{4,12},{5,13},{6,14},{7,15},{8,0},{9,1},... | collective-permute-start | bytes 231560 | tf_op jit(solution)/shard_map/ppermute | solution.py:8
  112.1 1.5 %copy-start.6 = (bf16[2,96,384]{2,1,0:T(8,128)(2,1)S(1)}, bf16[2,96,384]{2,1,0:T(8,128)(2,1)}, u32[]{:S(2)}) copy-start(bf16[2,96,384]{2,1,0:T(8,128)(2,1)} %param.15) | copy-start | bytes 442372
  112.1 1.5 %copy-start.8 = (bf16[2,384,96]{1,2,0:T(8,128)(2,1)S(1)}, bf16[2,384,96]{1,2,0:T(8,128)(2,1)}, u32[]{:S(2)}) copy-start(bf16[2,384,96]{1,2,0:T(8,128)(2,1)} %param.13) | copy-start | bytes 442372
where the time goes:
time: 124 us; the launch traced here: 123 us
  other arithmetic  55.1 us (44%)
  waiting for transfers between devices  33.9 us (27%)
  local copies, waits for them, and re-layouts  14.1 us (11%)
  starting transfers between devices  10.7 us (9%)
  matrix products  9.1 us (7%)
    reduce_sum x2, other arithmetic, compute(): mean = jnp.mean(conv, axis=0)  43.1 us
    ppermute x8, waiting for transfers between devices, swapped(): lax.ppermute(value, axis, [(i, i ^ 1 << bit) for i in range(lax.axis_size...  33.8 us
    ppermute x2, starting transfers between devices, extended_2(): lax.ppermute(head, axis, [((i + 1) % count, i) for i in range(count)])  9.49 us
    dot_general x2, matrix products, compute(): jnp.dot(wb, hidden, preferred_element_type=jnp.float32)  9.1 us
    reshape x2, local copies, waits for them, and re-layouts, compute(): jnp.dot(wb, hidden, preferred_element_type=jnp.float32)  4.52 us
    convert_element_type x2, other arithmetic, compute(): (mask_wide.astype(jnp.float32)[None] * (center.astype(jnp.float32) + oute...  3.51 us
    reduce_sum x2, other arithmetic, compute(): var = jnp.mean(cent * cent, axis=0)  3.26 us
    dot_general x1, local copies, waits for them, and re-layouts, compute(): jnp.dot(wb, hidden, preferred_element_type=jnp.float32)  2.88 us
  transfers between devices with their start and end apart: 12, of which 8 were waited for; matrix products, arithmetic and copies ran while one was open for 1% of the time, Pallas kernels for 0%

commit v1 on v0

v1 whole, which is shorter than its diff:
```python
import functools

import jax
import jax.numpy as jnp
from jax import lax
from jax.experimental import pallas as pl
from jax.experimental.pallas import tpu as pltpu
from jax.sharding import PartitionSpec as P

F32 = jnp.float32
BF16 = jnp.bfloat16
GROUP = 8
FOLD = 4


def roll(x, shift):
    return pltpu.roll(x, shift % x.shape[-1], axis=x.ndim - 1)


def lanes_of(shape):
    return lax.broadcasted_iota(jnp.int32, shape, len(shape) - 1)


def shifted(cells, halo, lane, d):
    width = cells.shape[-1]
    if d == 0:
        return cells
    beyond = lane < d if d > 0 else lane >= width + d
    return roll(jnp.where(beyond, halo, cells), -d)


def pack_edges(state, pack_ref, top_ref):
    tiles, rows, width = pack_ref.shape
    groups = width // GROUP
    lane = lanes_of((rows, width))

    @pl.loop(0, tiles)
    def _(tile):
        acc = jnp.zeros((rows, width), F32)
        for g in range(groups):
            cells = state[pl.ds((tile * groups + g) * rows, rows), :]
            inside = (lane >= g * GROUP) & (lane < (g + 1) * GROUP)
            acc = jnp.where(inside, roll(cells, g * GROUP + 3), acc)
        pack_ref[tile] = acc.astype(BF16)

    channels = top_ref.shape[1]
    for k in range(3):
        top_ref[k] = state[pl.ds(rows - 1 - k, channels, stride=rows), :].astype(BF16)


def start_kernel(field_ref, mask_ref, pack_ref, top_ref, state):
    channels, rows, width = field_ref.shape
    mask = mask_ref[...].astype(F32)

    @pl.loop(0, channels)
    def _(c):
        state[pl.ds(c * rows, rows), :] = field_ref[c].astype(F32) * mask

    pack_edges(state, pack_ref, top_ref)


def exchange_kernel(n, pack_ref, top_ref, west, east, ftop, feast, fwest, send, recv):
    me = lax.axis_index("zonal")
    rows = pack_ref.shape[1]
    right, left = lax.rem(me + 1, n), lax.rem(me + n - 1, n)
    across = n - 1 - me
    a_east, a_west = lax.rem(across + 1, n), lax.rem(across + n - 1, n)
    barrier = pltpu.get_barrier_semaphore()

    def greet(device):
        pl.semaphore_signal(
            barrier, inc=1, device_id={"zonal": device}, device_id_type=pl.DeviceIdType.MESH
        )

    for device in (right, left, across):
        greet(device)

    @pl.when(a_east != me)
    def _():
        greet(a_east)

    @pl.when(a_west != me)
    def _():
        greet(a_west)

    alone = jnp.where(a_east == me, 1, 0) + jnp.where(a_west == me, 1, 0)
    pl.semaphore_wait(barrier, 5 - alone)

    def copy(src, dst, slot, device):
        return pltpu.make_async_remote_copy(
            src_ref=src,
            dst_ref=dst,
            send_sem=send.at[slot],
            recv_sem=recv.at[slot],
            device_id={"zonal": device},
            device_id_type=pl.DeviceIdType.MESH,
        )

    edge = pack_ref.at[:, pl.ds(rows // 2, rows // 2), :]
    copies = [
        copy(top_ref, ftop, 2, across),
        copy(pack_ref, west, 0, right),
        copy(pack_ref, east, 1, left),
    ]
    for each in copies:
        each.start()
    for slot, device, dst in ((3, a_east, feast), (4, a_west, fwest)):

        @pl.when(device != me)
        def _():
            copy(edge, dst, slot, device).start()

        @pl.when(device == me)
        def _():
            pltpu.make_async_copy(edge, dst, recv.at[slot]).start()

    for slot, device, dst in ((3, a_east, feast), (4, a_west, fwest)):

        @pl.when(device != me)
        def _():
            copy(edge, dst, slot, device).wait()

        @pl.when(device == me)
        def _():
            pltpu.make_async_copy(edge, dst, recv.at[slot]).wait()

    for each in copies:
        each.wait()


def block_kernel(
    block, last, step, state_ref, mask_ref, west, east, ftop, feast, fwest, dw_ref, gain_ref,
    shift_ref, wa_ref, ba_ref, wb_ref, out_ref, *rest,
):
    pack_ref, top_ref = (None, None) if last else rest[:2]
    state, conv, t_low, t_high, north_halo, north = rest[-6:]
    channels, rows, width = state_ref.shape
    tiles = west.shape[0]
    groups = width // GROUP
    taps = dw_ref.shape[1]
    hidden_units = wa_ref.shape[1]
    lane = lanes_of((rows, width))
    maskf = mask_ref[...].astype(F32)

    tap = lax.broadcasted_iota(jnp.int32, (taps, 2 * width), 0)
    col = lax.broadcasted_iota(jnp.int32, (taps, 2 * width), 1)
    p, q = tap // 7, tap % 7
    main = 7 * rows
    beyond = col - main
    hit = jnp.where(
        col < main,
        jnp.where(col // rows == q, col % rows + 3 - p, -1),
        jnp.where(
            (beyond // FOLD == q) & (beyond % FOLD < 3), rows + 3 + beyond % FOLD - p, -1
        ),
    )
    weights = jnp.transpose(dw_ref[block]).astype(BF16)
    for r in range(rows):
        pick = jnp.where(hit == r, 1.0, 0.0).astype(BF16)
        band = jnp.dot(weights, pick, preferred_element_type=F32)
        t_low[pl.ds(r, channels, stride=rows), :] = band[:, :width]
        t_high[pl.ds(r, channels, stride=rows), :] = band[:, width:]

    half = rows // 2
    lane_half = lanes_of((half, width))

    @pl.loop(0, tiles)
    def _(tile):
        both = jnp.where(
            lane_half % GROUP >= 3, feast[tile].astype(F32), fwest[tile].astype(F32)
        )
        for g in range(groups):
            north_halo[pl.ds((tile * groups + g) * half, half), :] = roll(both, -(g * GROUP + 3))

    north[...] = jnp.zeros_like(north)
    flip = jnp.where(
        lax.broadcasted_iota(jnp.int32, (width, width), 0) + lanes_of((width, width)) == width - 1,
        1.0,
        0.0,
    ).astype(BF16)
    lane_c = lanes_of((channels, width))
    for k in range(3):
        halo = north_halo[pl.ds(half - 1 - k, channels, stride=half), :].astype(BF16)
        halo = jnp.dot(halo, flip, preferred_element_type=F32)
        cells = jnp.dot(ftop[k], flip, preferred_element_type=F32)
        for j in range(7):
            north[pl.ds(j * FOLD + k, channels, stride=rows), :] = shifted(
                cells, halo, lane_c, j - 3
            )

    @pl.loop(0, tiles)
    def _(tile):
        both = jnp.where(lane % GROUP >= 3, east[tile].astype(F32), west[tile].astype(F32))
        for g in range(groups):
            c = tile * groups + g
            at = pl.ds(c * rows, rows)
            cells = state_ref[c].astype(F32) * maskf
            state[at, :] = cells
            halo = roll(both, -(g * GROUP + 3))
            parts = [shifted(cells, halo, lane, j - 3).astype(BF16) for j in range(7)]
            parts.append(north[at, :].astype(BF16))
            band = jnp.concatenate([t_low[at, :], t_high[at, :]], axis=1).astype(BF16)
            conv[at, :] = jnp.dot(
                band, jnp.concatenate(parts, axis=0), preferred_element_type=F32
            )

    gain = jnp.transpose(jnp.broadcast_to(gain_ref[block : block + 1], (width, channels)))
    shift = jnp.transpose(jnp.broadcast_to(shift_ref[block : block + 1], (width, channels)))
    bias = jnp.transpose(jnp.broadcast_to(ba_ref[block : block + 1], (width, hidden_units)))
    bias = jnp.concatenate([bias] * step, axis=1)
    wa, wb = wa_ref[block], wb_ref[block]

    @pl.loop(0, rows // step)
    def _(index):
        normed = []
        for k in range(step):
            y = conv[pl.ds(index * step + k, channels, stride=rows), :]
            mean = jnp.sum(y, axis=0, keepdims=True) * (1.0 / channels)
            cent = y - mean
            var = jnp.sum(cent * cent, axis=0, keepdims=True) * (1.0 / channels)
            normed.append((cent * lax.rsqrt(var + 1e-06) * gain + shift).astype(BF16))
        v = jnp.dot(wa, jnp.concatenate(normed, axis=1), preferred_element_type=F32) + bias
        k0 = 0.7978845608028654
        th = jnp.tanh(v * (k0 + (k0 * 0.044715) * (v * v)))
        twice = (v + v * th).astype(BF16)
        outer = 0.5 * jnp.dot(wb, twice, preferred_element_type=F32)
        for k in range(step):
            at = pl.ds(index * step + k, channels, stride=rows)
            keep = mask_ref[pl.ds(index * step + k, 1), :].astype(F32)
            res = keep * (state[at, :] + outer[:, k * width : (k + 1) * width])
            state[at, :] = res.astype(BF16).astype(F32)

    @pl.loop(0, channels)
    def _(c):
        out_ref[c] = state[pl.ds(c * rows, rows), :].astype(BF16)

    if not last:
        pack_edges(state, pack_ref, top_ref)


VMEM = pl.BlockSpec(memory_space=pltpu.VMEM)
LIMIT = 56 * 1024 * 1024


def local(field, land_mask, dw_weight, ln_gain, ln_shift, w_in, b_in, w_out):
    channels, rows, width = field.shape
    blocks = dw_weight.shape[0]
    n = lax.axis_size("zonal")
    tiles = channels * GROUP // width
    packed = (
        jax.ShapeDtypeStruct((tiles, rows, width), BF16),
        jax.ShapeDtypeStruct((3, channels, width), BF16),
    )
    half = jax.ShapeDtypeStruct((tiles, rows // 2, width), BF16)
    flat = pltpu.VMEM((channels * rows, width), F32)
    pack, top = pl.pallas_call(
        start_kernel,
        out_shape=packed,
        in_specs=[VMEM] * 2,
        out_specs=(VMEM,) * 2,
        scratch_shapes=[flat],
        compiler_params=pltpu.CompilerParams(vmem_limit_bytes=LIMIT),
        name="start",
    )(field, land_mask)
    state = field
    for block in range(blocks):
        last = block == blocks - 1
        halos = pl.pallas_call(
            functools.partial(exchange_kernel, n),
            out_shape=(packed[0], packed[0], packed[1], half, half),
            in_specs=[VMEM] * 2,
            out_specs=(VMEM,) * 5,
            scratch_shapes=[pltpu.SemaphoreType.DMA((5,)), pltpu.SemaphoreType.DMA((5,))],
            compiler_params=pltpu.CompilerParams(collective_id=block, has_side_effects=True),
            name=f"exchange{block}",
        )(pack, top)
        outs = (jax.ShapeDtypeStruct(field.shape, BF16),) + (() if last else packed)
        res = pl.pallas_call(
            functools.partial(block_kernel, block, last, 4),
            out_shape=outs,
            in_specs=[VMEM] * 13,
            out_specs=(VMEM,) * len(outs),
            scratch_shapes=[
                flat,
                flat,
                flat,
                flat,
                pltpu.VMEM((channels * rows // 2, width), F32),
                flat,
            ],
            compiler_params=pltpu.CompilerParams(vmem_limit_bytes=LIMIT),
            name=f"block{block}",
        )(state, land_mask, *halos, dw_weight, ln_gain, ln_shift, w_in, b_in, w_out)
        state = res[0]
        if not last:
            pack, top = res[1:]
    return state


def solution(mesh):
    placed = (P("groups", None, "zonal"), P(None, "zonal"), P(), P(), P(), P(), P(), P())
    return jax.shard_map(
        local, mesh=mesh, in_specs=placed, out_specs=P("groups", None, "zonal"), check_vma=False
    )
```

time: 124 us -> 67.1 us (0.54)
  Pallas kernels: 0 us -> 64.2 us
  other arithmetic: 55.1 us -> 0 us
  waiting for transfers between devices: 33.9 us -> 0 us
  local copies, waits for them, and re-layouts: 14.1 us -> 2.25 us
  starting transfers between devices: 10.7 us -> 0 us
  matrix products: 9.1 us -> 0 us
    pallas_call x0 -> x5, Pallas kernels: none -> 64.2 us  [the longest x2 38.5 us: local(): pl.pallas_call(functools.partial(block_kernel, block, last, 4), out_shape...]
    reduce_sum x4 -> x0, other arithmetic: 46.4 us -> none  [the longest x2 43.1 us: compute(): mean = jnp.mean(conv, axis=0)]
    ppermute x12 -> x0, waiting for transfers between devices: 33.9 us -> none  [the longest x8 33.8 us: swapped(): lax.ppermute(value, axis, [(i, i ^ 1 << bit) for i in range(lax.axis_size...]
    ppermute x12 -> x0, starting transfers between devices: 10.7 us -> none  [the longest x2 9.49 us: extended_2(): lax.ppermute(head, axis, [((i + 1) % count, i) for i in range(count)])]
    dot_general x2 -> x0, matrix products: 9.1 us -> none  [compute(): jnp.dot(wb, hidden, preferred_element_type=jnp.float32)]
    convert_element_type x6 -> x0, other arithmetic: 7.15 us -> none  [the longest x2 3.51 us: compute(): (mask_wide.astype(jnp.float32)[None] * (center.astype(jnp.float32) + oute...]
    reshape x3 -> x0, local copies, waits for them, and re-layouts: 5.71 us -> none  [the longest x2 4.52 us: compute(): jnp.dot(wb, hidden, preferred_element_type=jnp.float32)]
    dot_general x1 -> x0, local copies, waits for them, and re-layouts: 2.88 us -> none  [compute(): jnp.dot(wb, hidden, preferred_element_type=jnp.float32)]
  transfers between devices with their start and end apart: 12 -> 0, of which waited for: 8 -> 0; matrix products, arithmetic and copies ran while one was open for 1% -> 0% of each run, Pallas kernels for 0% -> 0%
where the time goes in v1:
time: 67.1 us; the launch traced here: 66.4 us
  Pallas kernels  64.2 us (96%)
  local copies, waits for them, and re-layouts  2.25 us (3%)
    pallas_call x2, Pallas kernels, local(): pl.pallas_call(functools.partial(block_kernel, block, last, 4), out_shape...  38.5 us
    pallas_call x2, Pallas kernels, local(): pl.pallas_call(functools.partial(exchange_kernel, n), out_shape=(packed[0...  22.5 us
    pallas_call x1, Pallas kernels, local(): pl.pallas_call(start_kernel, out_shape=packed, in_specs=[VMEM] * 2, out_s...  3.19 us
    unnamed x4, local copies, waits for them, and re-layouts  2.25 us

profile of v1, /device:TPU:0, one launch (start us, length us, event | category | flops | bytes accessed | tf_op | source)
XLA Modules:
  0.0 66.4 jit_solution(15311899484113313201)
XLA Ops:
  0.0 1.4 %copy.9.dw_ref = f32[2,49,96]{2,1,0:T(8,128)} copy(f32[2,49,96]{2,0,1:T(2,128)} %param.10) | data formatting | bytes 75264 | tf_op args[2]
  1.4 0.0 copy-start
  1.4 3.2 %start.1 = (bf16[6,32,128]{2,1,0:T(8,128)(2,1)}, bf16[3,96,128]{2,1,0:T(8,128)(2,1)}) custom-call(bf16[96,32,128]{2,1,0:T(8,128)(2,1)} %state_ref.1, s32[32,128]{1,0:T(8,128)} %mask_ref.5), custom_call_target="tpu_custom_call" | custom-call | tf_op jit(solution)/shard_map/start/pallas_call | solution.py:256
  4.6 12.1 %exchange0.1 = (bf16[6,32,128]{2,1,0:T(8,128)(2,1)}, bf16[6,32,128]{2,1,0:T(8,128)(2,1)}, bf16[3,96,128]{2,1,0:T(8,128)(2,1)}, bf16[6,16,128]{2,1,0:T(8,128)(2,1)}, bf16[6,16,128]{2,1,0:T(8,128)(2,1)}) custom-call(bf16[6,32,128]{2,1,0:T(8,128)(2,1)} %get-tuple-element.20.pack_ref, bf16[3,96,128]{2,1,0:T(8,128)(2,1)} %get-tuple-element.21.top_ref), custom_call_target="tpu_custom_call" | custom-call | tf_op jit(solution)/shard_map/exchange0/pallas_call | solution.py:268
  16.7 0.0 copy-done
  16.7 0.8 %copy.10.wa_ref = bf16[2,384,96]{2,1,0:T(8,128)(2,1)} copy(bf16[2,384,96]{1,2,0:T(8,128)(2,1)S(1)} %copy-done) | data formatting | bytes 294912 | tf_op args[5]
  17.5 19.5 %block0.1 = (bf16[96,32,128]{2,1,0:T(8,128)(2,1)}, bf16[6,32,128]{2,1,0:T(8,128)(2,1)}, bf16[3,96,128]{2,1,0:T(8,128)(2,1)}) custom-call(bf16[96,32,128]{2,1,0:T(8,128)(2,1)} %state_ref.1, s32[32,128]{1,0:T(8,128)} %mask_ref.5, bf16[6,32,128]{2,1,0:T(8,128)(2,1)} %get-tuple-element.22.west, bf16[6,32,128]{2,1,0:T(8,128)(2,1)} %get-tuple-element.23.east, ...), custom_call_target="tpu_custom_call" | custom-call | tf_op jit(solution)/shard_map/block0/pallas_call | solution.py:278
  37.1 10.4 %exchange1.1 = (bf16[6,32,128]{2,1,0:T(8,128)(2,1)}, bf16[6,32,128]{2,1,0:T(8,128)(2,1)}, bf16[3,96,128]{2,1,0:T(8,128)(2,1)}, bf16[6,16,128]{2,1,0:T(8,128)(2,1)}, bf16[6,16,128]{2,1,0:T(8,128)(2,1)}) custom-call(bf16[6,32,128]{2,1,0:T(8,128)(2,1)} %get-tuple-element.28.pack_ref, bf16[3,96,128]{2,1,0:T(8,128)(2,1)} %get-tuple-element.29.top_ref), custom_call_target="tpu_custom_call" | custom-call | tf_op jit(solution)/shard_map/exchange1/pallas_call | solution.py:268
  47.5 19.0 %block1.1 = bf16[96,32,128]{2,1,0:T(8,128)(2,1)} custom-call(bf16[96,32,128]{2,1,0:T(8,128)(2,1)} %get-tuple-element.27.state_ref, s32[32,128]{1,0:T(8,128)} %mask_ref.5, bf16[6,32,128]{2,1,0:T(8,128)(2,1)} %get-tuple-element.30.west, bf16[6,32,128]{2,1,0:T(8,128)(2,1)} %get-tuple-element.31.east, bf16[3,96,128]{2,1,0:T(8,128)(2,1)} %get-tuple-element.32.ftop, ...), custom_call_target="tpu_custom_call" | custom-call | tf_op jit(solution)/shard_map/block1/pallas_call | solution.py:278
Async XLA Ops:
  1.4 15.3 %copy-start = (bf16[2,384,96]{1,2,0:T(8,128)(2,1)S(1)}, bf16[2,384,96]{1,2,0:T(8,128)(2,1)}, u32[]{:S(2)}) copy-start(bf16[2,384,96]{1,2,0:T(8,128)(2,1)} %param.13) | copy-start | bytes 442372

commit v2 on v0

v2 whole, which is shorter than its diff:
```python
import functools

import jax
import jax.numpy as jnp
from jax import lax
from jax.experimental import pallas as pl
from jax.experimental.pallas import tpu as pltpu
from jax.sharding import PartitionSpec as P

F32 = jnp.float32
BF16 = jnp.bfloat16
GROUP = 8
FOLD = 6
TAIL = 4
STEP = 14
PAD = 1


def roll(x, shift):
    return pltpu.roll(x, shift % x.shape[-1], axis=x.ndim - 1)


def lanes_of(shape):
    return lax.broadcasted_iota(jnp.int32, shape, len(shape) - 1)


def shifted(cells, halo, lane, d):
    width = cells.shape[-1]
    if d == 0:
        return cells
    beyond = lane < d if d > 0 else lane >= width + d
    return roll(jnp.where(beyond, halo, cells), -d)


def kernel(
    n, field_ref, mask_ref, dw_ref, gain_ref, shift_ref, wa_ref, ba_ref, wb_ref, out_ref, state,
    conv, t_low, t_high, pack, top, edge, west, east, ftop, feast, fwest, expand,
    send, recv,
):
    channels, rows, width = field_ref.shape
    taps, blocks = dw_ref.shape[:2]
    hidden_units = wa_ref.shape[2]
    tiles = pack.shape[1]
    groups = width // GROUP
    deep = edge.shape[1]
    pitch = rows + PAD
    lane = lanes_of((rows, width))
    lane_c = lanes_of((channels, width))
    lane_e = lanes_of((deep, width))
    maskf = mask_ref[...].astype(F32)

    me = lax.axis_index("zonal")
    right, left = lax.rem(me + 1, n), lax.rem(me + n - 1, n)
    across = n - 1 - me
    a_east, a_west = lax.rem(across + 1, n), lax.rem(across + n - 1, n)
    barrier = pltpu.get_barrier_semaphore()

    def greet(device):
        pl.semaphore_signal(
            barrier, inc=1, device_id={"zonal": device}, device_id_type=pl.DeviceIdType.MESH
        )

    for device in (right, left, across):
        greet(device)

    @pl.when(a_east != me)
    def _():
        greet(a_east)

    @pl.when(a_west != me)
    def _():
        greet(a_west)

    def copy(src, dst, block, slot, device):
        return pltpu.make_async_remote_copy(
            src_ref=src.at[block],
            dst_ref=dst.at[block],
            send_sem=send.at[block, slot],
            recv_sem=recv.at[block, slot],
            device_id={"zonal": device},
            device_id_type=pl.DeviceIdType.MESH,
        )

    def sides(block):
        return copy(pack, west, block, 0, right), copy(pack, east, block, 1, left)

    def fold(block, act):
        for slot, device, dst in ((3, a_east, feast), (4, a_west, fwest)):

            @pl.when(device != me)
            def _():
                act(copy(edge, dst, block, slot, device))

            @pl.when(device == me)
            def _():
                act(
                    pltpu.make_async_copy(
                        edge.at[block], dst.at[block], recv.at[block, slot]
                    )
                )

        act(copy(top, ftop, block, 2, across))

    def row(r):
        return pl.ds(r, channels, stride=pitch)

    def pack_top(block):
        acc = jnp.zeros((deep, width), F32)
        for k in range(3):
            cells = state[row(rows - 1 - k), :]
            top[block, k] = cells.astype(BF16)
            for part in range(channels // deep):
                at = (k * (channels // deep) + part) * FOLD
                inside = (lane_e >= at) & (lane_e < at + FOLD)
                acc = jnp.where(inside, roll(cells[part * deep : (part + 1) * deep], at + 3), acc)
        edge[block] = acc.astype(BF16)

    def pack_side(block, tile, each):
        acc = jnp.zeros((rows, width), F32)
        for g in range(groups):
            inside = (lane >= g * GROUP) & (lane < (g + 1) * GROUP)
            acc = jnp.where(inside, roll(each(tile * groups + g), g * GROUP + 3), acc)
        pack[block, tile] = acc.astype(BF16)

    def send_all(block):
        for each in sides(block):
            each.start()
        fold(block, lambda c: c.start())

    def bands(weights):
        tap = lax.broadcasted_iota(jnp.int32, (taps, 2 * width), 0)
        col = lax.broadcasted_iota(jnp.int32, (taps, 2 * width), 1)
        p, q = tap // 7, tap % 7
        hit = jnp.where(col // rows == q, col % rows + 3 - p, -1)
        weights = weights.astype(BF16)
        for r in range(rows):
            pick = jnp.where(hit == r, 1.0, 0.0).astype(BF16)
            band = jnp.dot(weights, pick, preferred_element_type=F32)
            t_low[row(r), :] = band[:, :width]
            t_high[row(r), :] = band[:, width:]

    def add_north(block, weights):
        flip = jnp.where(
            lax.broadcasted_iota(jnp.int32, (width, width), 0) + lanes_of((width, width))
            == width - 1,
            1.0,
            0.0,
        ).astype(BF16)
        both = jnp.where(
            lane_e % FOLD >= 3, feast[block].astype(F32), fwest[block].astype(F32)
        )
        sums = [conv[row(rows - 3 + r), :] for r in range(3)]
        for k in range(3):
            parts = [
                roll(both, -((k * (channels // deep) + part) * FOLD + 3))
                for part in range(channels // deep)
            ]
            halo = jnp.dot(
                jnp.concatenate(parts, axis=0).astype(BF16), flip, preferred_element_type=F32
            )
            cells = jnp.dot(ftop[block, k], flip, preferred_element_type=F32)
            for q in range(7):
                moved = shifted(cells, halo, lane_c, q - 3)
                for r in range(k, 3):
                    at = 7 * (6 + k - r) + q
                    sums[r] = sums[r] + weights[:, at : at + 1] * moved
        for r in range(3):
            conv[row(rows - 3 + r), :] = sums[r]

    def all_columns(ref, block, size):
        return jnp.transpose(jnp.broadcast_to(ref[block : block + 1], (width, size)))

    def mlp(block, start, step):
        gain = all_columns(gain_ref, block, channels)
        shift = all_columns(shift_ref, block, channels)
        bias = jnp.concatenate([all_columns(ba_ref, block, hidden_units)] * step, axis=1)
        normed = []
        for k in range(step):
            y = conv[row(start + k), :]
            mean = jnp.sum(y, axis=0, keepdims=True) * (1.0 / channels)
            cent = y - mean
            var = jnp.sum(cent * cent, axis=0, keepdims=True) * (1.0 / channels)
            normed.append((cent * lax.rsqrt(var + 1e-06) * gain + shift).astype(BF16))
        v = jnp.dot(
            expand[block], jnp.concatenate(normed, axis=1), preferred_element_type=F32
        )
        v = v + bias
        k0 = 0.7978845608028654
        th = jnp.tanh(v * (k0 + (k0 * 0.044715) * (v * v)))
        twice = (v + v * th).astype(BF16)
        outer = 0.5 * jnp.dot(wb_ref[block], twice, preferred_element_type=F32)
        for k in range(step):
            keep = mask_ref[pl.ds(start + k, 1), :].astype(F32)
            res = keep * (state[row(start + k), :] + outer[:, k * width : (k + 1) * width])
            state[row(start + k), :] = res.astype(BF16).astype(F32)

    @pl.loop(0, tiles)
    def _(tile):
        def masked(c):
            cells = field_ref[c].astype(F32) * maskf
            state[pl.ds(c * pitch, rows), :] = cells
            return cells

        pack_side(0, tile, masked)

    pack_top(0)
    alone = jnp.where(a_east == me, 1, 0) + jnp.where(a_west == me, 1, 0)
    pl.semaphore_wait(barrier, 5 - alone)
    send_all(0)

    for block in range(blocks):
        weights = jnp.transpose(dw_ref[:, block, :])
        expand[block] = jnp.transpose(wa_ref[block])
        bands(weights)
        for each in sides(block):
            each.wait()

        @pl.loop(0, tiles)
        def _(tile):
            both = jnp.where(
                lane % GROUP >= 3, east[block, tile].astype(F32), west[block, tile].astype(F32)
            )
            for g in range(groups):
                c = tile * groups + g
                at = pl.ds(c * pitch, rows)
                cells = state[at, :]
                halo = roll(both, -(g * GROUP + 3))
                parts = [shifted(cells, halo, lane, j - 3).astype(BF16) for j in range(7)]
                band = jnp.concatenate([t_low[at, :], t_high[at, :]], axis=1).astype(BF16)
                conv[at, :] = jnp.dot(
                    band[:, : 7 * rows],
                    jnp.concatenate(parts, axis=0),
                    preferred_element_type=F32,
                )

        @pl.loop(0, (rows - TAIL) // STEP)
        def _(index):
            mlp(block, index * STEP, STEP)

        fold(block, lambda c: c.wait())
        add_north(block, weights)
        mlp(block, rows - TAIL, TAIL)

        if block < blocks - 1:

            @pl.loop(0, tiles)
            def _(tile):
                pack_side(block + 1, tile, lambda c: state[pl.ds(c * pitch, rows), :])

            pack_top(block + 1)
            send_all(block + 1)

    @pl.loop(0, channels)
    def _(c):
        out_ref[c] = state[pl.ds(c * pitch, rows), :].astype(BF16)


VMEM = pl.BlockSpec(memory_space=pltpu.VMEM)


def local(field, land_mask, dw_weight, ln_gain, ln_shift, w_in, b_in, w_out):
    channels, rows, width = field.shape
    blocks = dw_weight.shape[0]
    tiles = channels * GROUP // width
    flat = pltpu.VMEM((channels * (rows + PAD), width), F32)
    packed = pltpu.VMEM((blocks, tiles, rows, width), BF16)
    tops = pltpu.VMEM((blocks, 3, channels, width), BF16)
    edges = pltpu.VMEM((blocks, 16, width), BF16)
    return pl.pallas_call(
        functools.partial(kernel, lax.axis_size("zonal")),
        out_shape=jax.ShapeDtypeStruct(field.shape, BF16),
        in_specs=[VMEM] * 8,
        out_specs=VMEM,
        scratch_shapes=[
            flat,
            flat,
            flat,
            flat,
            packed,
            tops,
            edges,
            packed,
            packed,
            tops,
            edges,
            edges,
            pltpu.VMEM(w_in.shape, BF16),
            pltpu.SemaphoreType.DMA((blocks, 5)),
            pltpu.SemaphoreType.DMA((blocks, 5)),
        ],
        compiler_params=pltpu.CompilerParams(
            collective_id=0, has_side_effects=True, vmem_limit_bytes=56 * 1024 * 1024
        ),
        name="evolve",
    )(
        field,
        land_mask,
        jnp.swapaxes(dw_weight, 0, 1),
        ln_gain,
        ln_shift,
        jnp.swapaxes(w_in, 1, 2),
        b_in,
        w_out,
    )


def solution(mesh):
    placed = (P("groups", None, "zonal"), P(None, "zonal"), P(), P(), P(), P(), P(), P())
    return jax.shard_map(
        local, mesh=mesh, in_specs=placed, out_specs=P("groups", None, "zonal"), check_vma=False
    )
```

time: 124 us -> 35.8 us (0.29)
  other arithmetic: 55.1 us -> 0 us
  waiting for transfers between devices: 33.9 us -> 0 us
  Pallas kernels: 0 us -> 33.6 us
  local copies, waits for them, and re-layouts: 14.1 us -> 2.06 us
  starting transfers between devices: 10.7 us -> 0 us
  matrix products: 9.1 us -> 0 us
    reduce_sum x4 -> x0, other arithmetic: 46.4 us -> none  [the longest x2 43.1 us: compute(): mean = jnp.mean(conv, axis=0)]
    ppermute x12 -> x0, waiting for transfers between devices: 33.9 us -> none  [the longest x8 33.8 us: swapped(): lax.ppermute(value, axis, [(i, i ^ 1 << bit) for i in range(lax.axis_size...]
    pallas_call x0 -> x1, Pallas kernels: none -> 33.6 us  [local(): pl.pallas_call(functools.partial(kernel, lax.axis_size('zonal')), out_sha...]
    ppermute x12 -> x0, starting transfers between devices: 10.7 us -> none  [the longest x2 9.49 us: extended_2(): lax.ppermute(head, axis, [((i + 1) % count, i) for i in range(count)])]
    dot_general x2 -> x0, matrix products: 9.1 us -> none  [compute(): jnp.dot(wb, hidden, preferred_element_type=jnp.float32)]
    convert_element_type x6 -> x0, other arithmetic: 7.15 us -> none  [the longest x2 3.51 us: compute(): (mask_wide.astype(jnp.float32)[None] * (center.astype(jnp.float32) + oute...]
    reshape x3 -> x0, local copies, waits for them, and re-layouts: 5.71 us -> none  [the longest x2 4.52 us: compute(): jnp.dot(wb, hidden, preferred_element_type=jnp.float32)]
    dot_general x1 -> x0, local copies, waits for them, and re-layouts: 2.88 us -> none  [compute(): jnp.dot(wb, hidden, preferred_element_type=jnp.float32)]
  transfers between devices with their start and end apart: 12 -> 0, of which waited for: 8 -> 0; matrix products, arithmetic and copies ran while one was open for 1% -> 0% of each run, Pallas kernels for 0% -> 0%
where the time goes in v2:
time: 35.8 us; the launch traced here: 35.7 us
  Pallas kernels  33.6 us (94%)
  local copies, waits for them, and re-layouts  2.06 us (6%)
    pallas_call x1, Pallas kernels, local(): pl.pallas_call(functools.partial(kernel, lax.axis_size('zonal')), out_sha...  33.6 us
    unnamed x1, local copies, waits for them, and re-layouts  2.06 us

profile of v2, /device:TPU:0, one launch (start us, length us, event | category | flops | bytes accessed | tf_op | source)
XLA Modules:
  0.0 35.7 jit_solution(7858391098433010521)
XLA Ops:
  0.0 33.6 %evolve.1 = bf16[96,32,128]{2,1,0:T(8,128)(2,1)} custom-call(bf16[96,32,128]{2,1,0:T(8,128)(2,1)} %field_ref.1, s32[32,128]{1,0:T(8,128)} %mask_ref.1, f32[49,2,96]{2,1,0:T(2,128)} %bitcast.3, f32[2,96]{1,0:T(2,128)} %gain_ref.1, f32[2,96]{1,0:T(2,128)} %shift_ref.1, bf16[2,96,384]{2,1,0:T(8,128)(2,1)} %bitcast.2, f32[2,384]{1,0:T(2,128)} %ba_ref.1, ...), custom_call_target="tpu_custom_call" | custom-call | tf_op jit(solution)/shard_map/evolve/pallas_call | solution.py:269
  33.6 2.1 %copy.10 = bf16[96,32,128]{2,1,0:T(8,128)(2,1)} copy(bf16[96,32,128]{2,1,0:T(8,128)(2,1)} %evolve.1) | data formatting | bytes 1572864

commit v3 on v2

--- a/solution.py
+++ b/solution.py
@@ -12,8 +12,8 @@
 GROUP = 8
 FOLD = 6
 TAIL = 4
-STEP = 14
-PAD = 1
+STEP = 28
+PAD = 4
 
 
 def roll(x, shift):
@@ -44,6 +44,8 @@
     groups = width // GROUP
     deep = edge.shape[1]
     pitch = rows + PAD
+    half = rows // 2
+    lane_h = lanes_of((half, width))
     lane = lanes_of((rows, width))
     lane_c = lanes_of((channels, width))
     lane_e = lanes_of((deep, width))
@@ -81,8 +83,19 @@
             device_id_type=pl.DeviceIdType.MESH,
         )
 
-    def sides(block):
-        return copy(pack, west, block, 0, right), copy(pack, east, block, 1, left)
+    def sides(block, part):
+        part_rows = pl.ds(part * half, half)
+        return [
+            pltpu.make_async_remote_copy(
+                src_ref=pack.at[block, :, part_rows, :],
+                dst_ref=dst.at[block, :, part_rows, :],
+                send_sem=send.at[block, slot],
+                recv_sem=recv.at[block, slot],
+                device_id={"zonal": device},
+                device_id_type=pl.DeviceIdType.MESH,
+            )
+            for dst, slot, device in ((west, 5 * part, right), (east, 5 * part + 1, left))
+        ]
 
     def fold(block, act):
         for slot, device, dst in ((3, a_east, feast), (4, a_west, fwest)):
@@ -115,17 +128,19 @@
                 acc = jnp.where(inside, roll(cells[part * deep : (part + 1) * deep], at + 3), acc)
         edge[block] = acc.astype(BF16)
 
-    def pack_side(block, tile, each):
-        acc = jnp.zeros((rows, width), F32)
-        for g in range(groups):
-            inside = (lane >= g * GROUP) & (lane < (g + 1) * GROUP)
-            acc = jnp.where(inside, roll(each(tile * groups + g), g * GROUP + 3), acc)
-        pack[block, tile] = acc.astype(BF16)
-
-    def send_all(block):
-        for each in sides(block):
+    def pack_side(block, part):
+        @pl.loop(0, tiles)
+        def _(tile):
+            acc = jnp.zeros((half, width), F32)
+            for g in range(groups):
+                inside = (lane_h >= g * GROUP) & (lane_h < (g + 1) * GROUP)
+                cells = state[pl.ds((tile * groups + g) * pitch + part * half, half), :]
+                acc = jnp.where(inside, roll(cells, g * GROUP + 3), acc)
+            pack[block, tile, pl.ds(part * half, half), :] = acc.astype(BF16)
+
+    def send_side(block, part):
+        for each in sides(block, part):
             each.start()
-        fold(block, lambda c: c.start())
 
     def bands(weights):
         tap = lax.broadcasted_iota(jnp.int32, (taps, 2 * width), 0)
@@ -190,29 +205,31 @@
         twice = (v + v * th).astype(BF16)
         outer = 0.5 * jnp.dot(wb_ref[block], twice, preferred_element_type=F32)
         for k in range(step):
-            keep = mask_ref[pl.ds(start + k, 1), :].astype(F32)
-            res = keep * (state[row(start + k), :] + outer[:, k * width : (k + 1) * width])
+            res = state[row(start + k), :] + outer[:, k * width : (k + 1) * width]
+            if block < blocks - 1:
+                res = mask_ref[pl.ds(start + k, 1), :].astype(F32) * res
             state[row(start + k), :] = res.astype(BF16).astype(F32)
 
     @pl.loop(0, tiles)
     def _(tile):
-        def masked(c):
-            cells = field_ref[c].astype(F32) * maskf
-            state[pl.ds(c * pitch, rows), :] = cells
-            return cells
-
-        pack_side(0, tile, masked)
-
-    pack_top(0)
+        for g in range(groups):
+            c = tile * groups + g
+            state[pl.ds(c * pitch, rows), :] = field_ref[c].astype(F32) * maskf
+
+    pack_side(0, 0)
+    pack_side(0, 1)
     alone = jnp.where(a_east == me, 1, 0) + jnp.where(a_west == me, 1, 0)
     pl.semaphore_wait(barrier, 5 - alone)
-    send_all(0)
+    send_side(0, 0)
+    send_side(0, 1)
+    pack_top(0)
+    fold(0, lambda c: c.start())
 
     for block in range(blocks):
         weights = jnp.transpose(dw_ref[:, block, :])
         expand[block] = jnp.transpose(wa_ref[block])
         bands(weights)
-        for each in sides(block):
+        for each in sides(block, 0) + sides(block, 1):
             each.wait()
 
         @pl.loop(0, tiles)
@@ -237,18 +254,18 @@
         def _(index):
             mlp(block, index * STEP, STEP)
 
+        if block < blocks - 1:
+            pack_side(block + 1, 0)
+            send_side(block + 1, 0)
         fold(block, lambda c: c.wait())
         add_north(block, weights)
         mlp(block, rows - TAIL, TAIL)
 
         if block < blocks - 1:
-
-            @pl.loop(0, tiles)
-            def _(tile):
-                pack_side(block + 1, tile, lambda c: state[pl.ds(c * pitch, rows), :])
-
+            pack_side(block + 1, 1)
+            send_side(block + 1, 1)
             pack_top(block + 1)
-            send_all(block + 1)
+            fold(block + 1, lambda c: c.start())
 
     @pl.loop(0, channels)
     def _(c):
@@ -266,7 +283,7 @@
     packed = pltpu.VMEM((blocks, tiles, rows, width), BF16)
     tops = pltpu.VMEM((blocks, 3, channels, width), BF16)
     edges = pltpu.VMEM((blocks, 16, width), BF16)
-    return pl.pallas_call(
+    unmasked = pl.pallas_call(
         functools.partial(kernel, lax.axis_size("zonal")),
         out_shape=jax.ShapeDtypeStruct(field.shape, BF16),
         in_specs=[VMEM] * 8,
@@ -285,8 +302,8 @@
             edges,
             edges,
             pltpu.VMEM(w_in.shape, BF16),
-            pltpu.SemaphoreType.DMA((blocks, 5)),
-            pltpu.SemaphoreType.DMA((blocks, 5)),
+            pltpu.SemaphoreType.DMA((blocks, 7)),
+            pltpu.SemaphoreType.DMA((blocks, 7)),
         ],
         compiler_params=pltpu.CompilerParams(
             collective_id=0, has_side_effects=True, vmem_limit_bytes=56 * 1024 * 1024
@@ -302,6 +319,7 @@
         b_in,
         w_out,
     )
+    return unmasked * land_mask.astype(BF16)[None]
 
 
 def solution(mesh):

time: 35.8 us -> 37 us (1.034)
  other arithmetic: 0 us -> 2.79 us
  local copies, waits for them, and re-layouts: 2.06 us -> 0 us
  Pallas kernels: 33.6 us -> 34 us
    mul x0 -> x1, other arithmetic: none -> 2.07 us  [local(): return unmasked * land_mask.astype(BF16)[None]]
    unnamed x1 -> x0, local copies, waits for them, and re-layouts: 2.06 us -> none
    convert_element_type x0 -> x1, other arithmetic: none -> 0.72 us  [local(): return unmasked * land_mask.astype(BF16)[None]]
where the time goes in v3:
time: 37 us; the launch traced here: 36.8 us
  Pallas kernels  34 us (92%)
  other arithmetic  2.79 us (8%)
    pallas_call x1, Pallas kernels, local(): pl.pallas_call(functools.partial(kernel, lax.axis_size('zonal')), out_sha...  34 us
    mul x1, other arithmetic, local(): return unmasked * land_mask.astype(BF16)[None]  2.07 us

profile of v3, /device:TPU:0, one launch (start us, length us, event | category | flops | bytes accessed | tf_op | source)
XLA Modules:
  0.0 36.8 jit_solution(15148906857282065546)
XLA Ops:
  0.0 0.7 %convert_element_type.3 = bf16[32,128]{1,0:T(8,128)(2,1)S(1)} convert(s32[32,128]{1,0:T(8,128)} %mask_ref.1) | non-fusion elementwise | flops 4096 | bytes 24576 | tf_op jit(solution)/shard_map/convert_element_type | solution.py:322
  0.7 34.0 %evolve.1 = bf16[96,32,128]{2,1,0:T(8,128)(2,1)} custom-call(bf16[96,32,128]{2,1,0:T(8,128)(2,1)} %field_ref.1, s32[32,128]{1,0:T(8,128)} %mask_ref.1, f32[49,2,96]{2,1,0:T(2,128)} %bitcast.3, f32[2,96]{1,0:T(2,128)} %gain_ref.1, f32[2,96]{1,0:T(2,128)} %shift_ref.1, bf16[2,96,384]{2,1,0:T(8,128)(2,1)} %bitcast.2, f32[2,384]{1,0:T(2,128)} %ba_ref.1, ...), custom_call_target="tpu_custom_call" | custom-call | tf_op jit(solution)/shard_map/evolve/pallas_call | solution.py:286
  34.7 2.1 %broadcast_multiply_fusion = bf16[96,32,128]{2,1,0:T(8,128)(2,1)} fusion(bf16[96,32,128]{2,1,0:T(8,128)(2,1)} %evolve.1, bf16[32,128]{1,0:T(8,128)(2,1)S(1)} %convert_element_type.3), kind=kLoop, calls=%fused_computation | loop fusion | flops 393216 | bytes 1581056 | tf_op jit(solution)/shard_map/mul | solution.py:322
